TPU v7x, 256 devices: a whole 4x4x8 slice. The times are simulated.
256 devices in a mesh: freq: 8 (over x, core), mode: 32 (over y, z).
Axes of the slice: x: 4, y: 4, z: 8, core: 2. Of those that a mesh axis runs over, the one named last changes fastest.
Arguments:
- mode_shapes: bfloat16 [6144, 12288], P(None, 'mode'), may hold values from -0.109375 to 0.109375
- modal_freq: float32 [12288], P('mode'), may hold values from 0.5 to 4
- damping: float32 [12288], P('mode'), may hold values from 0.05 to 0.2
- excitation: float32 [32], P('freq'), parts along dimension 0, may hold values from 0.5 to 4
- modal_load: float32 [12288, 32, 2, 64], P('mode', 'freq'), parts along dimension 1, may hold values from -6 to 6
- attach: int32 [32, 96], replicated, may hold values from 0 to 6143
- row_count: int32 [32], P('mode'), may hold values from 48 to 384, as said below
- otm: bfloat16 [32, 384, 96], P('mode'), may hold values from -0.625 to 0.625
Outputs:
- csd: bfloat16 [32, 32, 2, 384, 384], P('mode', 'freq'), parts along dimension 1
- joint_csd: bfloat16 [32, 32, 2, 128, 384], P('mode', 'freq'), parts along dimension 1
There are 8 independent parts, one for each index of `freq`. A program takes and returns all parts, laid end to end along the dimension named above; an argument that names none is the same for every part. Nothing has to cross between parts.
Inputs may be any that keep to these rules, and one draw needn't show every extreme that they name: `row_count`: at least one component has exactly 384 rows in every draw.
All inputs are finite; a program needn't handle non-finite values.
Results may differ from a plain program's by a relative error of at most 0.008.
Values may be sent and summed in bfloat16 or wider, within the bound.
A program may use at most 128 MiB of HBM per device.

v0:
```python
import jax
import jax.numpy as jnp
from jax import lax
from jax.sharding import PartitionSpec as P

CROSS = 128


def shifted(value, axis, steps):
    count = lax.axis_size(axis)
    initial, last = (max(0, -steps), min(count, count - steps))
    return lax.ppermute(value, axis, [(source, source + steps) for source in range(initial, last)])


def per_device(mode_shapes, modal_freq, damping, excitation, modal_load, attach, row_count, otm):
    comp_here = otm.shape[0]
    rows_max = otm.shape[1]
    att_len = otm.shape[2]
    lines = excitation.shape[0]
    width = modal_load.shape[3]
    columns = lines * 2 * width
    omega_sq = modal_freq * modal_freq
    real_part = omega_sq[:, None] - (excitation * excitation)[None, :]
    imag_part = 2.0 * damping[:, None] * modal_freq[:, None] * excitation[None, :]
    denom = real_part * real_part + imag_part * imag_part
    frf_re = (omega_sq[:, None] * real_part / denom)[:, :, None]
    frf_im = (-omega_sq[:, None] * imag_part / denom)[:, :, None]
    load_re = modal_load[:, :, 0, :]
    load_im = modal_load[:, :, 1, :]
    resp_re = frf_re * load_re - frf_im * load_im
    resp_im = frf_re * load_im + frf_im * load_re
    modal_resp = jnp.stack([resp_re, resp_im], axis=2).astype(jnp.bfloat16)
    modal_resp = modal_resp.reshape(modal_resp.shape[0], columns)
    flat_attach = attach.reshape(-1)
    own_start = lax.axis_index("mode") * (comp_here * att_len)
    band = lax.psum_scatter(
        jnp.dot(mode_shapes, modal_resp, preferred_element_type=jnp.float32),
        "mode",
        scatter_dimension=0,
        tiled=True,
    ).astype(jnp.bfloat16)
    whole = lax.all_gather(band, "mode", axis=0, tiled=True)
    index_rows = lax.dynamic_slice_in_dim(flat_attach, own_start, comp_here * att_len)
    picked = jnp.take(whole, index_rows, axis=0)
    picked = picked.reshape(comp_here, att_len, columns)
    row_mask = jnp.arange(rows_max, dtype=jnp.int32)[None, :] < row_count[:, None]
    masked_otm = jnp.where(row_mask[:, :, None], otm, jnp.zeros_like(otm))
    factor = jnp.einsum(
        "cra,caj->crj", masked_otm, picked, preferred_element_type=jnp.float32
    ).astype(jnp.bfloat16)
    zmat = factor.reshape(comp_here, rows_max, lines, 2 * width)
    wmat = jnp.concatenate([zmat[..., width:], -zmat[..., :width]], axis=-1)
    following = shifted(zmat[0], "mode", -1)
    partner = jnp.concatenate([zmat[1:], following[None]], axis=0)
    block = 128
    z_here = zmat[0]
    w_here = wmat[0]
    needed = (row_count[0] + block - 1) // block

    def block_step(step, buffer):
        z_rows = lax.dynamic_slice_in_dim(z_here, step * block, block, 0)
        w_rows = lax.dynamic_slice_in_dim(w_here, step * block, block, 0)
        part_re = (
            jnp.einsum("rfk,sfk->frs", z_rows, z_here, preferred_element_type=jnp.float32) / width
        )
        part_im = (
            jnp.einsum("rfk,sfk->frs", w_rows, z_here, preferred_element_type=jnp.float32) / width
        )
        value = jnp.stack([part_re, part_im], axis=1).astype(jnp.bfloat16)
        zero = jnp.zeros((), jnp.int32)
        return lax.dynamic_update_slice(
            buffer, value, (zero, zero, (step * block).astype(jnp.int32), zero)
        )

    empty = jnp.zeros((lines, 2, rows_max, rows_max), jnp.bfloat16)
    auto_blocks = [lax.fori_loop(0, needed, block_step, empty)]
    csd = jnp.stack(auto_blocks, axis=0)
    joint_re = (
        jnp.einsum("crfk,csfk->cfrs", zmat[:, :CROSS], partner, preferred_element_type=jnp.float32)
        / width
    )
    joint_im = (
        jnp.einsum("crfk,csfk->cfrs", wmat[:, :CROSS], partner, preferred_element_type=jnp.float32)
        / width
    )
    joint_csd = jnp.stack([joint_re, joint_im], axis=2).astype(jnp.bfloat16)
    return (csd, joint_csd)


def solution(mesh):
    return jax.shard_map(
        per_device,
        mesh=mesh,
        in_specs=(
            P(None, "mode"),
            P("mode"),
            P("mode"),
            P("freq"),
            P("mode", "freq", None, None),
            P(),
            P("mode"),
            P("mode", None, None),
        ),
        out_specs=(P("mode", "freq", None, None, None), P("mode", "freq", None, None, None)),
        check_vma=False,
    )
```

profile of v0, /device:TPU:4, one launch (start us, length us, event | category | flops | bytes accessed | tf_op | source)
XLA Modules:
  0.0 390.4 jit_solution(15512524188562069523)
XLA Ops:
  7.2 0.0 reduce-scatter.4.cloned.1.call-start
  7.2 0.7 mul.124
  7.9 0.7 multiply_multiply_fusion.2
  8.6 0.7 fusion.22
  9.4 1.2 subtract_convert_fusion
  10.7 8.7 %convolution_bitcast_fusion = f32[6144,512]{0,1:T(8,128)} fusion(bf16[384,512]{0,1:T(8,128)(2,1)S(1)} %bitcast.55, bf16[6144,384]{1,0:T(8,128)(2,1)} %param.10), kind=kOutput, calls=%fused_computation.13 | convolution fusion | flops 2415919104 | bytes 17694720 | tf_op jit(solution)/shard_map/dot_general | solution.py:37
  19.4 12.6 %copy.34 = f32[6144,512]{1,0:T(8,128)} copy(f32[6144,512]{0,1:T(8,128)} %convolution_bitcast_fusion) | data formatting | bytes 25165824
  32.0 0.0 copy-start.1
  32.0 0.0 copy-start
  32.0 0.0 reduce-scatter.4.cloned.1.call-update
  32.0 0.0 all-gather.2.cloned.1.call-start
  32.1 240.9 %reduce-scatter.4.cloned.1.call-done = f32[192,512]{1,0:T(8,128)} async-done(((f32[6144,512]{1,0:T(8,128)}), f32[192,512]{1,0:T(8,128)}) %reduce-scatter.4.cloned.1.call-update) | async-done | bytes 393232 | tf_op jit(solution)/shard_map/reduce_scatter | solution.py:36
  273.0 1.7 convert_element_type.23
  274.7 0.0 all-gather.2.cloned.1.call-update
  275.3 0.0 copy-done.1
  275.4 0.1 reshape.261
  275.4 0.1 compare_and_fusion
  275.5 87.6 %all-gather.2.cloned.1.call-done = bf16[6144,512]{1,0:T(8,128)(2,1)} async-done(((bf16[192,512]{1,0:T(8,128)(2,1)}), bf16[6144,512]{1,0:T(8,128)(2,1)}) %all-gather.2.cloned.1.call-update) | async-done | bytes 6291472 | tf_op jit(solution)/shard_map/all_gather | solution.py:42
  363.1 4.4 %gather_fusion = bf16[96,512]{1,0:T(8,128)(2,1)S(1)} fusion(bf16[6144,512]{1,0:T(8,128)(2,1)} %all-gather.2.cloned.1.call-done, s32[1024]{0:T(1024)S(1)} %pad_clamp_fusion), kind=kCustom, calls=%fused_computation | custom fusion | bytes 196992 | tf_op jit(solution)/shard_map/jit(_take)/gather | solution.py:44
  367.5 0.0 copy-done
  367.5 0.3 convolution_convert_fusion
  367.9 0.1 reshape.262
  368.0 0.8 copy_bitcast_fusion
  368.8 0.4 fusion.28
  369.1 0.1 copy.38
  369.2 0.1 copy_negate_fusion
  369.3 1.3 collective-permute-start
  370.6 0.2 maximum_bitcast_fusion
  370.8 1.6 broadcast_in_dim.21.clone
  372.4 3.7 while.10
  372.4 1.3 fusion.46
  373.7 1.4 fusion.47
  375.1 1.0 copy_dynamic-update-slice_fusion.2
  376.1 5.7 %collective-permute-done = bf16[384,4,128]{2,0,1:T(8,128)(2,1)S(1)} collective-permute-done((bf16[384,4,128]{2,0,1:T(8,128)(2,1)}, bf16[384,4,128]{2,0,1:T(8,128)(2,1)S(1)}, u32[]{:S(2)}, u32[]{:S(2)}) %collective-permute-start) | collective-permute-done | bytes 393248 | tf_op jit(solution)/shard_map/ppermute | solution.py:12
  381.9 0.3 fusion.10
  382.2 0.3 fusion.11
  382.5 0.1 pad_maximum_fusion.1
  382.6 1.0 copy.33
  (4 shorter events, 0.1 us)
Async XLA Ops:
  7.2 265.8 %reduce-scatter.4.cloned.1.call-start = ((), (), s32[]{:S(2)}) async-start(), calls=%async_computation.2 | async-start | bytes 12976128 | tf_op jit(solution)/shard_map/reduce_scatter | solution.py:36
  32.0 243.4 %copy-start.1 = (s32[32,96]{1,0:T(8,128)S(1)}, s32[32,96]{1,0:T(8,128)}, u32[]{:S(2)}) copy-start(s32[32,96]{1,0:T(8,128)} %param.15) | copy-start | bytes 36868
  32.0 335.5 %copy-start = (bf16[1,384,96]{1,2,0:T(8,128)(2,1)S(1)}, bf16[1,384,96]{1,2,0:T(8,128)(2,1)}, u32[]{:S(2)}) copy-start(bf16[1,384,96]{1,2,0:T(8,128)(2,1)} %param.17) | copy-start | bytes 221188
  32.0 331.1 %all-gather.2.cloned.1.call-start = ((), (), s32[]{:S(2)}) async-start(), calls=%async_computation.1 | async-start | bytes 6488064 | tf_op jit(solution)/shard_map/all_gather | solution.py:42
  369.3 12.6 %collective-permute-start = (bf16[384,4,128]{2,0,1:T(8,128)(2,1)}, bf16[384,4,128]{2,0,1:T(8,128)(2,1)S(1)}, u32[]{:S(2)}, u32[]{:S(2)}) collective-permute-start(bf16[384,4,128]{2,0,1:T(8,128)(2,1)} %copy_bitcast_fusion), channel_id=1, source_target_pairs={{1,0},{2,1},{3,2},{4,3},{5,4},{6,5},{7,6},{8,7},{9,8},{10,9},{11,1... | collective-permute-start | bytes 1179656 | tf_op jit(solution)/shard_map/ppermute | solution.py:12
Sparse Core Ops, SparseCore 0:
  32.1 240.8 reduce-scatter.3
  276.1 86.9 all-gather.1
where the time goes:
time: 394 us; the launch traced here: 390 us
  waiting for transfers between devices  334 us (85%)
  local copies, waits for them, and re-layouts  21 us (5%)
  between operations  14.8 us (4%)
  matrix products  12.4 us (3%)
  other arithmetic  6.59 us (2%)
    reduce_scatter x1, waiting for transfers between devices, per_device(): lax.psum_scatter(jnp.dot(mode_shapes, modal_resp, preferred_element_type=...  241 us
    all_gather x1, waiting for transfers between devices, per_device(): whole = lax.all_gather(band, 'mode', axis=0, tiled=True)  87.6 us
    unnamed x7, local copies, waits for them, and re-layouts  13.6 us
    dot_general x1, matrix products, per_device(): jnp.dot(mode_shapes, modal_resp, preferred_element_type=jnp.float32)  8.73 us
  transfers between devices with their start and end apart: 3, of which 3 were waited for; matrix products, arithmetic and copies ran while one was open for 1% of the time, Pallas kernels for 0%

commit v1 on v0

v1 whole, which is shorter than its diff:
```python
import functools

import jax
import jax.numpy as jnp
from jax import lax
from jax.experimental import pallas as pl
from jax.experimental.pallas import tpu as pltpu
from jax.sharding import PartitionSpec as P

MESH = pl.DeviceIdType.MESH
F32, BF16 = jnp.float32, jnp.bfloat16
NY, NZ = 4, 8
COMPS, ATT, LINES = 32, 96, 4
CROSS = 128
CHUNKS = (("z", 0, 24), ("z", 24, 24), ("y", 48, 24), ("y", 72, 24))
SIZE = {"y": NY, "z": NZ}


def partial_kernel(freq_ref, damp_ref, exc_ref, load_ref, attach_ref, shapes_ref, out_ref, held, resp, whole, sems):
    pieces = sems.shape[0]
    rows = held.shape[0] // pieces
    copies = []
    for piece in range(pieces):
        part = pl.ds(piece * rows, rows)
        copies.append(pltpu.make_async_copy(shapes_ref.at[part], held.at[part], sems.at[piece]))
        copies[-1].start()
    omega = freq_ref[...]
    omega_sq = omega * omega
    for line in range(LINES):
        exc = exc_ref[line]
        a = omega_sq - exc * exc
        b = 2.0 * damp_ref[...] * omega * exc
        denom = a * a + b * b
        frf_re = omega_sq * a / denom
        frf_im = -omega_sq * b / denom
        load_re = load_ref[pl.ds(line * 128, 64), :]
        load_im = load_ref[pl.ds(line * 128 + 64, 64), :]
        resp[pl.ds(line * 128, 64), :] = (frf_re * load_re - frf_im * load_im).astype(BF16)
        resp[pl.ds(line * 128 + 64, 64), :] = (frf_re * load_im + frf_im * load_re).astype(BF16)
    for piece in range(pieces):
        copies[piece].wait()
    steps = 16
    tall = held.shape[0] // steps

    def product(step, carry):
        base = pl.multiple_of(step * tall, tall)
        block = lax.dot_general(
            held[pl.ds(base, tall), :], resp[...], (((1,), (1,)), ((), ())), preferred_element_type=F32
        )
        for line in range(LINES):
            whole[pl.ds(base * LINES + line, tall, stride=LINES), :] = block[:, line * 128 : line * 128 + 128]
        return carry

    lax.fori_loop(0, steps, product, 0)
    unroll = 16

    def gather(step, carry):
        for k in range(unroll):
            row = step * unroll + k
            source = attach_ref[row] * LINES
            out_ref[pl.ds(pl.multiple_of(row * LINES, LINES), LINES), :] = whole[
                pl.ds(pl.multiple_of(source, LINES), LINES), :
            ]
        return carry

    lax.fori_loop(0, COMPS * ATT // unroll, gather, 0)


def plan():
    place, total = {}, 0
    for index, (first, start, rows) in enumerate(CHUNKS):
        order = (first, "y" if first == "z" else "z")
        for phase in range(2):
            n = SIZE[order[phase]]
            inner = SIZE[order[1]] if phase == 0 else 1
            for step in range(n // 2, 0, -1):
                size = inner * rows * LINES
                if step == n // 2:
                    size //= 2
                for side in range(2):
                    place[(index, phase, side, step)] = (len(place), total, size)
                    total += size
    return place, total


PLACE, TOTAL = plan()
ORDER = None


def default_order():
    events = []
    for index, (first, start, rows) in enumerate(CHUNKS):
        order = (first, "y" if first == "z" else "z")
        clock = 0.0
        for phase in range(2):
            n = SIZE[order[phase]]
            big = (14.0 / 4 if order[0] == "z" else 12.0 / 2) if phase == 0 else 2.0
            for step in range(n // 2, -1, -1):
                events.append((clock + 0.01 * index, index, phase, step))
                clock += big * (0.5 if step == n // 2 else 1.0) if step else 0.0
    return [e[1:] for e in sorted(events)]


def reduce_kernel(part_ref, otm_ref, count_ref, own_ref, next_ref, otm_out, otm_next_out,
                  sent, got, held, total, final, otm_mine, otm_got, pick, pick_got, wide,
                  send_sems, recv_sems):
    me = lax.axis_index("mode")
    y, z = me // NZ, lax.rem(me, NZ)
    at = {"y": y, "z": z}

    def device(axis, offset):
        if axis == "z":
            return y * NZ + lax.rem(z + offset + NZ, NZ)
        return lax.rem(y + offset + NY, NY) * NZ + z

    before = lax.rem(me + NY * NZ - 1, NY * NZ)
    after = lax.rem(me + 1, NY * NZ)
    barrier = pltpu.get_barrier_semaphore()
    for peer in (device("z", 1), device("z", -1), device("y", 1), device("y", -1), before, after):
        pl.semaphore_signal(barrier, inc=1, device_id={"mode": peer}, device_id_type=MESH)
    pl.semaphore_wait(barrier, 6)

    count = count_ref[0]
    keep = lax.broadcasted_iota(jnp.int32, otm_ref.shape, 1) < count
    masked = jnp.where(keep, otm_ref[...].astype(F32), 0.0).astype(BF16)
    otm_mine[...] = masked
    otm_out[...] = masked
    base = len(PLACE)
    otm_copy = pltpu.make_async_remote_copy(
        src_ref=otm_mine, dst_ref=otm_got, send_sem=send_sems.at[base], recv_sem=recv_sems.at[base],
        device_id={"mode": before}, device_id_type=MESH)
    otm_copy.start()

    copies, tails = {}, []

    def event(index, phase, step):
        first, start, rows = CHUNKS[index]
        order = (first, "y" if first == "z" else "z")
        axis, other = order[phase], order[1 - phase]
        n = SIZE[axis]
        inner = SIZE[order[1]] if phase == 0 else 1
        tall = rows * LINES

        def own(dest, item):
            if phase == 0:
                unit = item * NZ + dest if axis == "z" else dest * NZ + item
                return part_ref[pl.ds(pl.multiple_of(unit * (ATT * LINES) + start * LINES, 8), tall), :]
            return held[pl.ds(pl.multiple_of((index * NZ + dest) * 96, 8), tall), :]

        def rows_at(ref, offset, item):
            return ref.at[pl.ds(pl.multiple_of(offset + item * tall, 16), tall), :]

        if step == 0:
            places = [PLACE[(index, phase, side, 1)] for side in range(2)]
            for side in range(2):
                copies[(index, phase, side, 1)].wait_recv()

            def add(item, carry):
                value = own(at[axis], item)
                for side in range(2):
                    value = value + rows_at(got, places[side][1], item)[...].astype(F32)
                if phase == 0:
                    held[pl.ds(pl.multiple_of((index * NZ + item) * 96, 8), tall), :] = value
                else:
                    pick[pl.ds(start * LINES, tall), :] = value.astype(BF16)
                return carry

            if phase == 0:
                lax.fori_loop(0, inner, add, 0)
            else:
                add(0, 0)
                slot = base + 1 + index
                part = pl.ds(start * LINES, tall)
                copy = pltpu.make_async_remote_copy(
                    src_ref=pick.at[part], dst_ref=pick_got.at[part], send_sem=send_sems.at[slot],
                    recv_sem=recv_sems.at[slot], device_id={"mode": before}, device_id_type=MESH)
                copy.start()
                tails.append(copy)
            return

        for side in range(2):
            sign = 1 if side == 0 else -1
            number, offset, size = PLACE[(index, phase, side, step)]
            dest = lax.rem(at[axis] + sign * step + n, n)
            if step == n // 2:
                if inner == 1:
                    half = tall // 2
                    value = held[pl.ds(pl.multiple_of((index * NZ + dest) * 96 + side * half, 8), half), :]
                    sent[pl.ds(offset, half), :] = value.astype(BF16)
                else:
                    def fill(item, carry):
                        rows_at(sent, offset, item)[...] = own(dest, item + side * (inner // 2)).astype(BF16)
                        return carry

                    lax.fori_loop(0, inner // 2, fill, 0)
            else:
                copies[(index, phase, side, step + 1)].wait_recv()
                arrived = PLACE[(index, phase, side, step + 1)][1]
                if step + 1 == n // 2:
                    if inner == 1:
                        half = tall // 2
                        lo, hi = (0, half) if side == 0 else (half, 0)
                        with_, without = (0, half) if side == 0 else (half, 0)
                        src = (index * NZ + dest) * 96
                        value = held[pl.ds(pl.multiple_of(src + with_, 8), half), :]
                        value = value + got[pl.ds(arrived, half), :].astype(F32)
                        sent[pl.ds(offset + with_, half), :] = value.astype(BF16)
                        value = held[pl.ds(pl.multiple_of(src + without, 8), half), :]
                        sent[pl.ds(offset + without, half), :] = value.astype(BF16)
                    else:
                        half = inner // 2

                        def fill(item, carry):
                            value = own(dest, item + side * half) + rows_at(got, arrived, item)[...].astype(F32)
                            rows_at(sent, offset, item + side * half)[...] = value.astype(BF16)
                            rows_at(sent, offset, item + (1 - side) * half)[...] = own(
                                dest, item + (1 - side) * half
                            ).astype(BF16)
                            return carry

                        lax.fori_loop(0, half, fill, 0)
                else:
                    def fill(item, carry):
                        value = own(dest, item) + rows_at(got, arrived, item)[...].astype(F32)
                        rows_at(sent, offset, item)[...] = value.astype(BF16)
                        return carry

                    if inner == 1:
                        fill(0, 0)
                    else:
                        lax.fori_loop(0, inner, fill, 0)
            part = pl.ds(offset, size)
            copy = pltpu.make_async_remote_copy(
                src_ref=sent.at[part], dst_ref=got.at[part], send_sem=send_sems.at[number],
                recv_sem=recv_sems.at[number], device_id={"mode": device(axis, sign)}, device_id_type=MESH)
            copy.start()
            copies[(index, phase, side, step)] = copy

    for index, phase, step in default_order():
        event(index, phase, step)
    for line in range(LINES):
        pass
    wide[...] = pick[...].astype(F32)
    for line in range(LINES):
        own_ref[line] = wide[pl.ds(line, ATT, stride=LINES), :].astype(BF16)
    otm_copy.wait_recv()
    otm_next_out[...] = otm_got[...]
    for copy in tails:
        copy.wait_recv()
    wide[...] = jnp.where(me == NY * NZ - 1, 0.0, pick_got[...].astype(F32))
    for line in range(LINES):
        next_ref[line] = wide[pl.ds(line, ATT, stride=LINES), :].astype(BF16)
    for copy in [*copies.values(), *tails, otm_copy]:
        copy.wait_send()


def spectra_kernel(own_ref, next_ref, otm_ref, otm_next_ref, csd_ref, joint_ref):
    def factor(otm, picked):
        return lax.dot_general(otm, picked, (((0,), (0,)), ((), ())), preferred_element_type=F32).astype(BF16)

    def spectra(left, right):
        return lax.dot_general(left, right, (((1,), (1,)), ((), ())), preferred_element_type=F32) * (1.0 / 64.0)

    z_here = factor(otm_ref[...], own_ref[0])
    z_next = factor(otm_next_ref[...], next_ref[0])
    lane = lax.broadcasted_iota(jnp.int32, z_here.shape, 1)
    turned = pltpu.roll(z_here.astype(F32), 64, 1)
    w_here = jnp.where(lane < 64, turned, -turned).astype(BF16)
    csd_ref[0, 0, 0] = spectra(z_here, z_here).astype(BF16)
    csd_ref[0, 0, 1] = spectra(w_here, z_here).astype(BF16)
    joint_ref[0, 0, 0] = spectra(z_here[:CROSS], z_next).astype(BF16)
    joint_ref[0, 0, 1] = spectra(w_here[:CROSS], z_next).astype(BF16)


def per_device(mode_shapes, modal_freq, damping, excitation, modal_load, attach, row_count, otm):
    iface, modes = mode_shapes.shape
    rows_max, width = otm.shape[1], modal_load.shape[3]
    columns = LINES * 2 * width
    load = modal_load.transpose(1, 2, 3, 0).reshape(columns, modes)
    otm_t = otm[0].T
    vmem = pl.BlockSpec(memory_space=pltpu.VMEM)
    smem = pl.BlockSpec(memory_space=pltpu.SMEM)
    partial = pl.pallas_call(
        partial_kernel,
        out_shape=jax.ShapeDtypeStruct((COMPS * ATT * LINES, 128), F32),
        in_specs=[vmem, vmem, smem, vmem, smem, pl.BlockSpec(memory_space=pl.ANY)],
        out_specs=vmem,
        scratch_shapes=[
            pltpu.VMEM((iface, modes), BF16),
            pltpu.VMEM((columns, modes), BF16),
            pltpu.VMEM((iface * LINES, 128), F32),
            pltpu.SemaphoreType.DMA((8,)),
        ],
        compiler_params=pltpu.CompilerParams(vmem_limit_bytes=48 << 20),
        name="partial",
    )(modal_freq[None, :], damping[None, :], excitation, load, attach.reshape(-1), mode_shapes)
    slots = len(PLACE) + 1 + len(CHUNKS)
    own, following, otm_here, otm_next = pl.pallas_call(
        reduce_kernel,
        out_shape=[
            jax.ShapeDtypeStruct((LINES, ATT, 128), BF16),
            jax.ShapeDtypeStruct((LINES, ATT, 128), BF16),
            jax.ShapeDtypeStruct((ATT, rows_max), BF16),
            jax.ShapeDtypeStruct((ATT, rows_max), BF16),
        ],
        in_specs=[vmem, vmem, smem],
        out_specs=[vmem] * 4,
        scratch_shapes=[
            pltpu.VMEM((TOTAL, 128), BF16),
            pltpu.VMEM((TOTAL, 128), BF16),
            pltpu.VMEM((len(CHUNKS) * NZ * 96, 128), F32),
            pltpu.VMEM((8, 128), F32),
            pltpu.VMEM((8, 128), F32),
            pltpu.VMEM((ATT, rows_max), BF16),
            pltpu.VMEM((ATT, rows_max), BF16),
            pltpu.VMEM((ATT * LINES, 128), BF16),
            pltpu.VMEM((ATT * LINES, 128), BF16),
            pltpu.VMEM((ATT * LINES, 128), F32),
            pltpu.SemaphoreType.DMA((slots,)),
            pltpu.SemaphoreType.DMA((slots,)),
        ],
        compiler_params=pltpu.CompilerParams(
            vmem_limit_bytes=40 << 20, collective_id=0, has_side_effects=True
        ),
        name="reduce",
    )(partial, otm_t, row_count)
    by_line = pl.BlockSpec((1, ATT, 128), lambda f: (f, 0, 0))
    whole = pl.BlockSpec((ATT, rows_max), lambda f: (0, 0))
    return tuple(
        pl.pallas_call(
            spectra_kernel,
            grid=(LINES,),
            out_shape=[
                jax.ShapeDtypeStruct((1, LINES, 2, rows_max, rows_max), BF16),
                jax.ShapeDtypeStruct((1, LINES, 2, CROSS, rows_max), BF16),
            ],
            in_specs=[by_line, by_line, whole, whole],
            out_specs=[
                pl.BlockSpec((1, 1, 2, rows_max, rows_max), lambda f: (0, f, 0, 0, 0)),
                pl.BlockSpec((1, 1, 2, CROSS, rows_max), lambda f: (0, f, 0, 0, 0)),
            ],
            name="spectra",
        )(own, following, otm_here, otm_next)
    )


def solution(mesh):
    return jax.shard_map(
        per_device,
        mesh=mesh,
        in_specs=(
            P(None, "mode"),
            P("mode"),
            P("mode"),
            P("freq"),
            P("mode", "freq", None, None),
            P(),
            P("mode"),
            P("mode", None, None),
        ),
        out_specs=(P("mode", "freq", None, None, None), P("mode", "freq", None, None, None)),
        check_vma=False,
    )
```

time: 394 us -> 76 us (0.19)
  waiting for transfers between devices: 334 us -> 0 us
  Pallas kernels: 0 us -> 62.5 us
  between operations: 14.8 us -> 1.33 us
  matrix products: 12.4 us -> 0 us
  local copies, waits for them, and re-layouts: 21 us -> 11.6 us
  other arithmetic: 6.59 us -> 0 us
    reduce_scatter x1 -> x0, waiting for transfers between devices: 241 us -> none  [per_device(): lax.psum_scatter(jnp.dot(mode_shapes, modal_resp, preferred_element_type=...]
    all_gather x1 -> x0, waiting for transfers between devices: 87.6 us -> none  [per_device(): whole = lax.all_gather(band, 'mode', axis=0, tiled=True)]
    pallas_call x0 -> x3, Pallas kernels: none -> 62.5 us  [the longest x1 42.8 us: per_device(): pl.pallas_call(reduce_kernel, out_shape=[jax.ShapeDtypeStruct((LINES, ATT...]
    dot_general x6 -> x0, matrix products: 12.4 us -> none  [the longest x1 8.73 us: per_device(): jnp.dot(mode_shapes, modal_resp, preferred_element_type=jnp.float32)]
    ppermute x1 -> x0, waiting for transfers between devices: 5.72 us -> none  [shifted(): lax.ppermute(value, axis, [(source, source + steps) for source in range(i...]
    gather x1 -> x0, local copies, waits for them, and re-layouts: 4.39 us -> none  [per_device(): picked = jnp.take(whole, index_rows, axis=0)]
    unnamed x7 -> x18, local copies, waits for them, and re-layouts: 13.6 us -> 9.45 us
  transfers between devices with their start and end apart: 3 -> 0, of which waited for: 3 -> 0; matrix products, arithmetic and copies ran while one was open for 1% -> 0% of each run, Pallas kernels for 0% -> 0%
where the time goes in v1:
time: 76 us; the launch traced here: 75.4 us
  Pallas kernels  62.5 us (82%)
  local copies, waits for them, and re-layouts  11.6 us (15%)
  between operations  1.33 us (2%)
    pallas_call x1, Pallas kernels, per_device(): pl.pallas_call(reduce_kernel, out_shape=[jax.ShapeDtypeStruct((LINES, ATT...  42.8 us
    pallas_call x1, Pallas kernels, per_device(): pl.pallas_call(partial_kernel, out_shape=jax.ShapeDtypeStruct((COMPS * AT...  15.2 us
    unnamed x18, local copies, waits for them, and re-layouts  9.45 us
    pallas_call x1, Pallas kernels, per_device(): pl.pallas_call(spectra_kernel, grid=(LINES,), out_shape=[jax.ShapeDtypeSt...  4.55 us

profile of v1, /device:TPU:4, one launch (start us, length us, event | category | flops | bytes accessed | tf_op | source)
XLA Modules:
  0.0 75.4 jit_solution(6774790379322026909)
XLA Ops:
  1.3 0.7 broadcast_in_dim.6.freq_ref
  2.0 0.7 broadcast_in_dim.7.damp_ref
  2.6 0.8 %reshape.11.attach_ref = s32[3072]{0:T(1024)S(1)} reshape(s32[32,96]{1,0:T(8,128)} %param.13) | data formatting | bytes 24576 | tf_op jit(solution)/shard_map/reshape | solution.py:296
  3.4 0.0 copy-start.1
  3.4 2.3 %copy-done.1 = bf16[6144,384]{1,0:T(8,128)(2,1)S(1)} copy-done((bf16[6144,384]{1,0:T(8,128)(2,1)S(1)}, bf16[6144,384]{1,0:T(8,128)(2,1)}, u32[]{:S(2)}) %copy-start.1) | copy-done | bytes 4718616
  5.8 0.0 copy-start.2
  5.8 1.1 %copy-done.2 = f32[384,4,2,64]{0,3,2,1:T(8,128)S(1)} copy-done((f32[384,4,2,64]{0,3,2,1:T(8,128)S(1)}, f32[384,4,2,64]{0,3,2,1:T(8,128)}, u32[]{:S(2)}) %copy-start.2) | copy-done | bytes 786456
  6.9 0.0 copy-start.8
  6.9 0.7 copy-done.8
  7.6 0.0 copy-start.7
  7.6 15.2 %partial.1.part_ref = f32[12288,128]{1,0:T(8,128)} custom-call(f32[1,384]{1,0:T(1,128)S(1)} %broadcast_in_dim.6.freq_ref, f32[1,384]{1,0:T(1,128)S(1)} %broadcast_in_dim.7.damp_ref, f32[4]{0:T(128)S(1)} %copy-done.8, f32[512,384]{1,0:T(8,128)S(1)} %bitcast.6, s32[3072]{0:T(1024)S(1)} %reshape.11.attach_ref, bf16[6144,384]{1,0:T(8,128)(2,1)S(1)} %copy-done.1), custom_call_target="tpu_custom_call" | custom-call | tf_op jit(solution)/shard_map/partial/pallas_call | solution.py:283
  22.8 0.0 copy-done.7
  22.8 0.0 copy-start
  22.8 2.8 %copy-done = f32[12288,128]{1,0:T(8,128)S(1)} copy-done((f32[12288,128]{1,0:T(8,128)S(1)}, f32[12288,128]{1,0:T(8,128)}, u32[]{:S(2)}) %copy-start) | copy-done | bytes 6291480
  25.5 42.8 %reduce.1 = (bf16[4,96,128]{2,1,0:T(8,128)(2,1)S(1)}, bf16[4,96,128]{2,1,0:T(8,128)(2,1)S(1)}, bf16[96,384]{1,0:T(8,128)(2,1)S(1)}, bf16[96,384]{1,0:T(8,128)(2,1)S(1)}) custom-call(f32[12288,128]{1,0:T(8,128)S(1)} %copy-done, bf16[96,384]{1,0:T(8,128)(2,1)S(1)} %bitcast.7, s32[1]{0:T(128)S(6)} %copy.10.count_ref), custom_call_target="tpu_custom_call" | custom-call | tf_op jit(solution)/shard_map/reduce/pallas_call | solution.py:298
  68.3 0.0 copy-start.3
  68.3 0.6 copy-done.3
  69.0 0.0 copy-start.4
  69.0 0.6 copy-done.4
  69.6 0.0 copy-start.5
  69.6 0.6 copy-done.5
  70.2 0.0 copy-start.6
  70.2 0.6 copy-done.6
  70.9 4.5 %spectra.1 = (bf16[1,4,2,384,384]{4,3,2,1,0:T(8,128)(2,1)}, bf16[1,4,2,128,384]{4,3,2,1,0:T(8,128)(2,1)}) custom-call(bf16[4,96,128]{2,1,0:T(8,128)(2,1)} %copy-done.3, bf16[4,96,128]{2,1,0:T(8,128)(2,1)} %copy-done.4, bf16[96,384]{1,0:T(8,128)(2,1)} %copy-done.5, bf16[96,384]{1,0:T(8,128)(2,1)} %copy-done.6), custom_call_target="tpu_custom_call" | custom-call | tf_op jit(solution)/shard_map/spectra/pallas_call | solution.py:330
Async XLA Ops:
  3.4 2.3 %copy-start.1 = (bf16[6144,384]{1,0:T(8,128)(2,1)S(1)}, bf16[6144,384]{1,0:T(8,128)(2,1)}, u32[]{:S(2)}) copy-start(bf16[6144,384]{1,0:T(8,128)(2,1)} %shapes_ref.1) | copy-start | bytes 14155780
  5.8 1.1 %copy-start.2 = (f32[384,4,2,64]{0,3,2,1:T(8,128)S(1)}, f32[384,4,2,64]{0,3,2,1:T(8,128)}, u32[]{:S(2)}) copy-start(f32[384,4,2,64]{0,3,2,1:T(8,128)} %param.12) | copy-start | bytes 2359300
  6.9 0.7 copy-start.8
  7.6 15.2 %copy-start.7 = (bf16[1,384,96]{1,2,0:T(8,128)(2,1)S(1)}, bf16[1,384,96]{1,2,0:T(8,128)(2,1)}, u32[]{:S(2)}) copy-start(bf16[1,384,96]{1,2,0:T(8,128)(2,1)} %param.15) | copy-start | bytes 221188
  22.8 2.8 %copy-start = (f32[12288,128]{1,0:T(8,128)S(1)}, f32[12288,128]{1,0:T(8,128)}, u32[]{:S(2)}) copy-start(f32[12288,128]{1,0:T(8,128)} %partial.1.part_ref) | copy-start | bytes 18874372
  68.3 0.6 copy-start.3
  69.0 0.6 copy-start.4
  69.6 0.6 copy-start.5
  70.2 0.6 copy-start.6

commit v2 on v0

v2 whole, which is shorter than its diff:
```python
import jax
import jax.numpy as jnp
from jax import lax
from jax.experimental import pallas as pl
from jax.experimental.pallas import tpu as pltpu
from jax.sharding import PartitionSpec as P

MESH = pl.DeviceIdType.MESH
F32, BF16 = jnp.float32, jnp.bfloat16
NY, NZ = 4, 8
SIZE = {"y": NY, "z": NZ}
OTHER = {"y": "z", "z": "y"}
COMPS, ATT, LINES, CROSS = 32, 96, 4, 128
PIECES = 4
CHUNKS = (
    ("z", 0, 16), ("z", 16, 16), ("y", 32, 12), ("y", 44, 28), ("y", 72, 24),
)
ORDER = (
    (0, 4), (1, 4), (2, 2), (3, 2), (4, 2), (0, 3), (1, 3), (2, 1), (3, 1), (0, 2), (4, 1), (1, 2), (2, 0),
    (0, 1), (1, 1), (3, 0), (2, -1), (0, 0), (1, 0), (4, 0), (0, -1), (1, -1), (3, -1), (4, -1),
)
TALL = max(rows for _, _, rows in CHUNKS) * LINES


def plan():
    place, total = {}, 0
    for index, (first, _, rows) in enumerate(CHUNKS):
        n, m, tall = SIZE[first], SIZE[OTHER[first]], rows * LINES
        for hop in range(n // 2, 0, -1):
            size = m * tall // (2 if hop == n // 2 else 1)
            for side in range(2):
                place[(index, hop, side)] = (len(place), total, size)
                total += size
        for step in range(1, m):
            place[(index, "direct", step)] = (len(place), total, tall)
            total += tall
    return place, total


PLACE, TOTAL = plan()
SLOTS = len(PLACE) + 1 + len(CHUNKS)


def kernel(freq_hbm, damp_hbm, exc_hbm, load_hbm, attach, count_smem, otm_hbm, shapes_hbm, csd_ref, joint_ref,
           freq, damp, exc_smem, load, otm, shapes, resp, whole, own, mine, sent, got,
           otm_got, pick, pick_got, wide, in_sems, send_sems, recv_sems):
    me = lax.axis_index("mode")
    at = {"y": me // NZ, "z": lax.rem(me, NZ)}

    def device(axis, offset):
        if axis == "z":
            return at["y"] * NZ + lax.rem(at["z"] + offset + NZ, NZ)
        return lax.rem(at["y"] + offset + NY, NY) * NZ + at["z"]

    before = lax.rem(me + NY * NZ - 1, NY * NZ)
    after = lax.rem(me + 1, NY * NZ)
    barrier = pltpu.get_barrier_semaphore()
    peers = [device("z", step) for step in range(1, NZ)] + [device("y", step) for step in range(1, NY)]
    for peer in (*peers, before, after):
        pl.semaphore_signal(barrier, inc=1, device_id={"mode": peer}, device_id_type=MESH)

    small = [(freq_hbm, freq), (damp_hbm, damp), (exc_hbm, exc_smem), (load_hbm, load), (otm_hbm, otm)]
    rows = shapes.shape[0] // PIECES
    parts = [pl.ds(piece * rows, rows) for piece in range(PIECES)]
    loads = [pltpu.make_async_copy(src, dst, in_sems.at[k]) for k, (src, dst) in enumerate(small)]
    loads += [
        pltpu.make_async_copy(shapes_hbm.at[part], shapes.at[part], in_sems.at[len(small) + k])
        for k, part in enumerate(parts)
    ]
    for copy in loads:
        copy.start()
    for copy in loads[:4]:
        copy.wait()
    omega = freq[...].reshape(1, -1)
    ratio = damp[...].reshape(1, -1)
    omega_sq = omega * omega
    for line in range(LINES):
        exc = exc_smem[line]
        a = omega_sq - exc * exc
        b = 2.0 * ratio * omega * exc
        denom = a * a + b * b
        frf_re = omega_sq * a / denom
        frf_im = -omega_sq * b / denom
        load_re = load[pl.ds(line * 128, 64), :]
        load_im = load[pl.ds(line * 128 + 64, 64), :]
        resp[pl.ds(line * 128, 64), :] = (frf_re * load_re - frf_im * load_im).astype(BF16)
        resp[pl.ds(line * 128 + 64, 64), :] = (frf_re * load_im + frf_im * load_re).astype(BF16)
    for piece in range(PIECES):
        loads[len(small) + piece].wait()
        block = lax.dot_general(
            shapes[parts[piece], :], resp[...], (((1,), (1,)), ((), ())), preferred_element_type=F32
        )
        for line in range(LINES):
            whole[pl.ds(piece * rows * LINES + line, rows, stride=LINES), :] = block[:, line * 128 : line * 128 + 128]
    loads[4].wait()
    keep = lax.broadcasted_iota(jnp.int32, otm.shape, 1) < count_smem[0]
    otm[...] = jnp.where(keep, otm[...].astype(F32), 0.0).astype(BF16)

    pl.semaphore_wait(barrier, len(peers) + 2)
    copies, tails = {}, []
    table = whole.reshape(whole.shape[0] // LINES, LINES, 128)

    def send(key, place, target, source=sent, dest=got):
        number, offset, size = place
        part = pl.ds(offset, size)
        copy = pltpu.make_async_remote_copy(
            src_ref=source.at[part], dst_ref=dest.at[part], send_sem=send_sems.at[number],
            recv_sem=recv_sems.at[number], device_id={"mode": target}, device_id_type=MESH)
        copy.start()
        copies[key] = copy
        return copy

    def event(index, hop):
        first, start, rows = CHUNKS[index]
        other = OTHER[first]
        n, m, tall = SIZE[first], SIZE[other], rows * LINES

        def block(offset, item):
            return pl.ds(pl.multiple_of(offset + item * tall, 16), tall)

        def gather(dest, item, slot):
            unit = item * NZ + dest if first == "z" else dest * NZ + item
            base = pl.multiple_of(slot * tall, 16)
            for row in range(rows):
                source = attach[unit, start + row]
                own[pl.ds(base + row * LINES, LINES), :] = table[source]

        if hop > 0:
            half = m // 2
            dests = [lax.rem(at[first] + (hop if side == 0 else n - hop), n) for side in range(2)]

            def fetch(low, high):
                def body(item, carry):
                    for side in range(2):
                        gather(dests[side], item + side * low, side * m + item + side * low)
                    return carry

                lax.fori_loop(0, high, body, 0)

            if hop == n // 2:
                fetch(half, half)
            else:
                fetch(0, m)
            for side in range(2):
                place = PLACE[(index, hop, side)]
                if hop == n // 2:
                    def fill(item, carry):
                        sent[block(place[1], item), :] = own[block(0, side * (m + half) + item), :].astype(BF16)
                        return carry

                    lax.fori_loop(0, half, fill, 0)
                else:
                    copies[(index, hop + 1, side)].wait_recv()
                    arrived = PLACE[(index, hop + 1, side)][1]
                    short = hop + 1 == n // 2
                    skip = side * half if short else 0

                    def fill(item, carry):
                        value = own[block(0, side * m + skip + item), :] + got[block(arrived, item), :].astype(F32)
                        sent[block(place[1], skip + item), :] = value.astype(BF16)
                        if short:
                            rest = (1 - side) * half + item
                            sent[block(place[1], rest), :] = own[block(0, side * m + rest), :].astype(BF16)
                        return carry

                    lax.fori_loop(0, half if short else m, fill, 0)
                send((index, hop, side), place, device(first, 1 if side == 0 else -1))
        elif hop == 0:
            def body(item, carry):
                gather(at[first], item, item)
                return carry

            lax.fori_loop(0, m, body, 0)
            arrived = [PLACE[(index, 1, side)][1] for side in range(2)]
            for side in range(2):
                copies[(index, 1, side)].wait_recv()

            def value(item):
                here = own[block(0, item), :]
                for side in range(2):
                    here = here + got[block(arrived[side], item), :].astype(F32)
                return here

            for step in sorted(range(1, m), key=lambda step: -min(step, m - step)):
                place = PLACE[(index, "direct", step)]
                sent[pl.ds(place[1], tall), :] = value(lax.rem(at[other] + step, m)).astype(BF16)
                send((index, "direct", step), place, device(other, step))
            mine[pl.ds(start * LINES, tall), :] = value(at[other])
        else:
            here = mine[pl.ds(start * LINES, tall), :]
            for step in range(1, m):
                copies[(index, "direct", step)].wait_recv()
                here = here + got[pl.ds(PLACE[(index, "direct", step)][1], tall), :].astype(F32)
            pick[pl.ds(start * LINES, tall), :] = here.astype(BF16)
            place = (len(PLACE) + 1 + index, start * LINES, tall)
            tails.append(send((index, "pick"), place, before, pick, pick_got))

    for number, (index, hop) in enumerate(ORDER):
        event(index, hop)
        if number == 4:
            otm_copy = pltpu.make_async_remote_copy(
                src_ref=otm, dst_ref=otm_got, send_sem=send_sems.at[len(PLACE)],
                recv_sem=recv_sems.at[len(PLACE)], device_id={"mode": before}, device_id_type=MESH)
            otm_copy.start()

    def factor(otm_ref, picked, line):
        rows = wide[pl.ds(line, ATT, stride=LINES), :].astype(BF16)
        return lax.dot_general(
            otm_ref[...], rows, (((0,), (0,)), ((), ())), preferred_element_type=F32
        ).astype(BF16)

    def spectra(left, right):
        return lax.dot_general(left, right, (((1,), (1,)), ((), ())), preferred_element_type=F32) * (1.0 / 64.0)

    wide[...] = pick[...].astype(F32)
    crossing = []
    for line in range(LINES):
        here = factor(otm, pick, line)
        lane = lax.broadcasted_iota(jnp.int32, here.shape, 1)
        turned = pltpu.roll(here.astype(F32), 64, 1)
        turned = jnp.where(lane < 64, turned, -turned).astype(BF16)
        csd_ref[0, line, 0] = spectra(here, here).astype(BF16)
        csd_ref[0, line, 1] = spectra(turned, here).astype(BF16)
        crossing.append((here[:CROSS], turned[:CROSS]))
    otm_copy.wait_recv()
    for copy in tails:
        copy.wait_recv()
    wide[...] = jnp.where(me == NY * NZ - 1, 0.0, pick_got[...].astype(F32))
    for line in range(LINES):
        following = factor(otm_got, pick_got, line)
        here, turned = crossing[line]
        joint_ref[0, line, 0] = spectra(here, following).astype(BF16)
        joint_ref[0, line, 1] = spectra(turned, following).astype(BF16)
    for copy in (*copies.values(), otm_copy):
        copy.wait_send()


def per_device(mode_shapes, modal_freq, damping, excitation, modal_load, attach, row_count, otm):
    iface, modes = mode_shapes.shape
    rows_max, width = otm.shape[1], modal_load.shape[3]
    columns = LINES * 2 * width
    vmem = pl.BlockSpec(memory_space=pltpu.VMEM)
    hbm = pl.BlockSpec(memory_space=pltpu.HBM)
    smem = pl.BlockSpec(memory_space=pltpu.SMEM)
    operands = (
        modal_freq,
        damping,
        excitation,
        modal_load.transpose(1, 2, 3, 0).reshape(columns, modes),
        attach,
        row_count,
        otm[0].T,
        mode_shapes,
    )
    return tuple(
        pl.pallas_call(
            kernel,
            out_shape=[
                jax.ShapeDtypeStruct((1, LINES, 2, rows_max, rows_max), BF16),
                jax.ShapeDtypeStruct((1, LINES, 2, CROSS, rows_max), BF16),
            ],
            in_specs=[hbm] * 4 + [smem] * 2 + [hbm] * 2,
            out_specs=[vmem] * 2,
            scratch_shapes=[
                pltpu.VMEM((modes,), F32),
                pltpu.VMEM((modes,), F32),
                pltpu.SMEM((LINES,), F32),
                pltpu.VMEM((columns, modes), F32),
                pltpu.VMEM((ATT, rows_max), BF16),
                pltpu.VMEM((iface, modes), BF16),
                pltpu.VMEM((columns, modes), BF16),
                pltpu.VMEM((iface * LINES, 128), F32),
                pltpu.VMEM((2 * NZ * TALL, 128), F32),
                pltpu.VMEM((ATT * LINES, 128), F32),
                pltpu.VMEM((TOTAL, 128), BF16),
                pltpu.VMEM((TOTAL, 128), BF16),
                pltpu.VMEM((ATT, rows_max), BF16),
                pltpu.VMEM((ATT * LINES, 128), BF16),
                pltpu.VMEM((ATT * LINES, 128), BF16),
                pltpu.VMEM((ATT * LINES, 128), F32),
                pltpu.SemaphoreType.DMA((5 + PIECES,)),
                pltpu.SemaphoreType.DMA((SLOTS,)),
                pltpu.SemaphoreType.DMA((SLOTS,)),
            ],
            compiler_params=pltpu.CompilerParams(
                vmem_limit_bytes=42 << 20, collective_id=0, has_side_effects=True
            ),
            name="loads",
        )(*(value if value is row_count or value is attach else pltpu.with_memory_space_constraint(value, pltpu.HBM) for value in operands))
    )


def solution(mesh):
    return jax.shard_map(
        per_device,
        mesh=mesh,
        in_specs=(
            P(None, "mode"),
            P("mode"),
            P("mode"),
            P("freq"),
            P("mode", "freq", None, None),
            P(),
            P("mode"),
            P("mode", None, None),
        ),
        out_specs=(P("mode", "freq", None, None, None), P("mode", "freq", None, None, None)),
        check_vma=False,
    )
```

time: 394 us -> 49.3 us (0.13)
  waiting for transfers between devices: 334 us -> 0 us
  Pallas kernels: 0 us -> 44.8 us
  local copies, waits for them, and re-layouts: 21 us -> 3 us
  between operations: 14.8 us -> 1.3 us
  matrix products: 12.4 us -> 0 us
  other arithmetic: 6.59 us -> 0 us
    reduce_scatter x1 -> x0, waiting for transfers between devices: 241 us -> none  [per_device(): lax.psum_scatter(jnp.dot(mode_shapes, modal_resp, preferred_element_type=...]
    all_gather x1 -> x0, waiting for transfers between devices: 87.6 us -> none  [per_device(): whole = lax.all_gather(band, 'mode', axis=0, tiled=True)]
    pallas_call x0 -> x1, Pallas kernels: none -> 44.8 us  [per_device(): pl.pallas_call(kernel, out_shape=[jax.ShapeDtypeStruct((1, LINES, 2, rows...]
    dot_general x6 -> x0, matrix products: 12.4 us -> none  [the longest x1 8.73 us: per_device(): jnp.dot(mode_shapes, modal_resp, preferred_element_type=jnp.float32)]
    unnamed x7 -> x4, local copies, waits for them, and re-layouts: 13.6 us -> 3 us
    ppermute x1 -> x0, waiting for transfers between devices: 5.72 us -> none  [shifted(): lax.ppermute(value, axis, [(source, source + steps) for source in range(i...]
    gather x1 -> x0, local copies, waits for them, and re-layouts: 4.39 us -> none  [per_device(): picked = jnp.take(whole, index_rows, axis=0)]
  transfers between devices with their start and end apart: 3 -> 0, of which waited for: 3 -> 0; matrix products, arithmetic and copies ran while one was open for 1% -> 0% of each run, Pallas kernels for 0% -> 0%
where the time goes in v2:
time: 49.3 us; the launch traced here: 49.1 us
  Pallas kernels  44.8 us (91%)
  local copies, waits for them, and re-layouts  3 us (6%)
  between operations  1.3 us (3%)
    pallas_call x1, Pallas kernels, per_device(): pl.pallas_call(kernel, out_shape=[jax.ShapeDtypeStruct((1, LINES, 2, rows...  44.8 us
    unnamed x4, local copies, waits for them, and re-layouts  3 us

profile of v2, /device:TPU:4, one launch (start us, length us, event | category | flops | bytes accessed | tf_op | source)
XLA Modules:
  0.0 49.1 jit_solution(12024096383260345731)
XLA Ops:
  1.3 0.0 copy-start
  1.3 0.7 %copy-done = s32[32,96]{1,0:T(8,128)S(1)} copy-done((s32[32,96]{1,0:T(8,128)S(1)}, s32[32,96]{1,0:T(8,128)}, u32[]{:S(2)}) %copy-start) | copy-done | bytes 12312
  2.0 44.8 %loads.1 = (bf16[1,4,2,384,384]{4,3,2,1,0:T(8,128)(2,1)S(1)}, bf16[1,4,2,128,384]{4,3,2,1,0:T(8,128)(2,1)S(1)}) custom-call(f32[384]{0:T(512)} %freq_hbm.1, f32[384]{0:T(512)} %damp_hbm.1, f32[4]{0:T(128)} %exc_hbm.1, f32[512,384]{1,0:T(8,128)} %bitcast.6, s32[32,96]{1,0:T(8,128)S(1)} %copy-done, s32[1]{0:T(128)S(6)} %copy.12.count_smem, ...), custom_call_target="tpu_custom_call" | custom-call | tf_op jit(solution)/shard_map/loads/pallas_call | solution.py:256
  46.8 1.4 %copy.13 = bf16[1,4,2,384,384]{4,3,2,1,0:T(8,128)(2,1)} copy(bf16[1,4,2,384,384]{4,3,2,1,0:T(8,128)(2,1)S(1)} %get-tuple-element.4) | data formatting | bytes 4718592
  48.3 0.9 %copy.14 = bf16[1,4,2,128,384]{4,3,2,1,0:T(8,128)(2,1)} copy(bf16[1,4,2,128,384]{4,3,2,1,0:T(8,128)(2,1)S(1)} %get-tuple-element.5) | data formatting | bytes 1572864
Async XLA Ops:
  1.3 0.7 %copy-start = (s32[32,96]{1,0:T(8,128)S(1)}, s32[32,96]{1,0:T(8,128)}, u32[]{:S(2)}) copy-start(s32[32,96]{1,0:T(8,128)} %attach.1) | copy-start | bytes 36868

commit v3 on v2

--- a/solution.py
+++ b/solution.py
@@ -41,8 +41,8 @@
 SLOTS = len(PLACE) + 1 + len(CHUNKS)
 
 
-def kernel(freq_hbm, damp_hbm, exc_hbm, load_hbm, attach, count_smem, otm_hbm, shapes_hbm, csd_ref, joint_ref,
-           freq, damp, exc_smem, load, otm, shapes, resp, whole, own, mine, sent, got,
+def kernel(freq_hbm, damp_hbm, exc_hbm, load_hbm, attach_hbm, count_hbm, otm_hbm, shapes_hbm, csd_ref, joint_ref,
+           freq, damp, exc_smem, load, attach, count_smem, otm, shapes, resp, whole, own, mine, sent, got,
            otm_got, pick, pick_got, wide, in_sems, send_sems, recv_sems):
     me = lax.axis_index("mode")
     at = {"y": me // NZ, "z": lax.rem(me, NZ)}
@@ -54,12 +54,8 @@
 
     before = lax.rem(me + NY * NZ - 1, NY * NZ)
     after = lax.rem(me + 1, NY * NZ)
-    barrier = pltpu.get_barrier_semaphore()
-    peers = [device("z", step) for step in range(1, NZ)] + [device("y", step) for step in range(1, NY)]
-    for peer in (*peers, before, after):
-        pl.semaphore_signal(barrier, inc=1, device_id={"mode": peer}, device_id_type=MESH)
-
-    small = [(freq_hbm, freq), (damp_hbm, damp), (exc_hbm, exc_smem), (load_hbm, load), (otm_hbm, otm)]
+    small = [(freq_hbm, freq), (damp_hbm, damp), (exc_hbm, exc_smem), (load_hbm, load), (count_hbm, count_smem),
+             (otm_hbm, otm), (attach_hbm, attach)]
     rows = shapes.shape[0] // PIECES
     parts = [pl.ds(piece * rows, rows) for piece in range(PIECES)]
     loads = [pltpu.make_async_copy(src, dst, in_sems.at[k]) for k, (src, dst) in enumerate(small)]
@@ -69,6 +65,10 @@
     ]
     for copy in loads:
         copy.start()
+    barrier = pltpu.get_barrier_semaphore()
+    peers = [device("z", step) for step in range(1, NZ)] + [device("y", step) for step in range(1, NY)]
+    for peer in (*peers, before, after):
+        pl.semaphore_signal(barrier, inc=1, device_id={"mode": peer}, device_id_type=MESH)
     for copy in loads[:4]:
         copy.wait()
     omega = freq[...].reshape(1, -1)
@@ -92,7 +92,8 @@
         )
         for line in range(LINES):
             whole[pl.ds(piece * rows * LINES + line, rows, stride=LINES), :] = block[:, line * 128 : line * 128 + 128]
-    loads[4].wait()
+    for copy in loads[4:7]:
+        copy.wait()
     keep = lax.broadcasted_iota(jnp.int32, otm.shape, 1) < count_smem[0]
     otm[...] = jnp.where(keep, otm[...].astype(F32), 0.0).astype(BF16)
 
@@ -235,13 +236,23 @@
         copy.wait_send()
 
 
+def store(csd_ref, joint_ref, csd_hbm, joint_hbm, sems):
+    copies = []
+    for line in range(LINES):
+        copies.append(pltpu.make_async_copy(csd_ref.at[0, line], csd_hbm.at[0, line], sems.at[2 * line]))
+        copies.append(pltpu.make_async_copy(joint_ref.at[0, line], joint_hbm.at[0, line], sems.at[2 * line + 1]))
+    for copy in copies:
+        copy.start()
+    for copy in copies:
+        copy.wait()
+
+
 def per_device(mode_shapes, modal_freq, damping, excitation, modal_load, attach, row_count, otm):
     iface, modes = mode_shapes.shape
     rows_max, width = otm.shape[1], modal_load.shape[3]
     columns = LINES * 2 * width
     vmem = pl.BlockSpec(memory_space=pltpu.VMEM)
     hbm = pl.BlockSpec(memory_space=pltpu.HBM)
-    smem = pl.BlockSpec(memory_space=pltpu.SMEM)
     operands = (
         modal_freq,
         damping,
@@ -252,20 +263,21 @@
         otm[0].T,
         mode_shapes,
     )
-    return tuple(
-        pl.pallas_call(
+    spectra = pl.pallas_call(
             kernel,
             out_shape=[
                 jax.ShapeDtypeStruct((1, LINES, 2, rows_max, rows_max), BF16),
                 jax.ShapeDtypeStruct((1, LINES, 2, CROSS, rows_max), BF16),
             ],
-            in_specs=[hbm] * 4 + [smem] * 2 + [hbm] * 2,
+            in_specs=[hbm] * 8,
             out_specs=[vmem] * 2,
             scratch_shapes=[
                 pltpu.VMEM((modes,), F32),
                 pltpu.VMEM((modes,), F32),
                 pltpu.SMEM((LINES,), F32),
                 pltpu.VMEM((columns, modes), F32),
+                pltpu.SMEM((COMPS, ATT), jnp.int32),
+                pltpu.SMEM((1,), jnp.int32),
                 pltpu.VMEM((ATT, rows_max), BF16),
                 pltpu.VMEM((iface, modes), BF16),
                 pltpu.VMEM((columns, modes), BF16),
@@ -278,7 +290,7 @@
                 pltpu.VMEM((ATT * LINES, 128), BF16),
                 pltpu.VMEM((ATT * LINES, 128), BF16),
                 pltpu.VMEM((ATT * LINES, 128), F32),
-                pltpu.SemaphoreType.DMA((5 + PIECES,)),
+                pltpu.SemaphoreType.DMA((7 + PIECES,)),
                 pltpu.SemaphoreType.DMA((SLOTS,)),
                 pltpu.SemaphoreType.DMA((SLOTS,)),
             ],
@@ -286,7 +298,17 @@
                 vmem_limit_bytes=42 << 20, collective_id=0, has_side_effects=True
             ),
             name="loads",
-        )(*(value if value is row_count or value is attach else pltpu.with_memory_space_constraint(value, pltpu.HBM) for value in operands))
+        )(*(value if value is row_count else pltpu.with_memory_space_constraint(value, pltpu.HBM) for value in operands))
+    return tuple(
+        pl.pallas_call(
+            store,
+            out_shape=[jax.ShapeDtypeStruct(value.shape, BF16) for value in spectra],
+            in_specs=[vmem] * 2,
+            out_specs=[hbm] * 2,
+            scratch_shapes=[pltpu.SemaphoreType.DMA((2 * LINES,))],
+            compiler_params=pltpu.CompilerParams(vmem_limit_bytes=1 << 20),
+            name="store",
+        )(*spectra)
     )
 
 

time: 49.3 us -> 47.2 us (0.957)
  local copies, waits for them, and re-layouts: 3 us -> 0 us
  Pallas kernels: 44.8 us -> 45.8 us
    unnamed x4 -> x0, local copies, waits for them, and re-layouts: 3 us -> none
    pallas_call x0 -> x1, Pallas kernels: none -> 1.72 us  [per_device(): pl.pallas_call(store, out_shape=[jax.ShapeDtypeStruct(value.shape, BF16)...]
    pallas_call x1, Pallas kernels: 44.8 us -> 44.1 us  [per_device(): pl.pallas_call(kernel, out_shape=[jax.ShapeDtypeStruct((1, LINES, 2, rows...]
where the time goes in v3:
time: 47.2 us; the launch traced here: 47.1 us
  Pallas kernels  45.8 us (97%)
  between operations  1.29 us (3%)
    pallas_call x1, Pallas kernels, per_device(): pl.pallas_call(kernel, out_shape=[jax.ShapeDtypeStruct((1, LINES, 2, rows...  44.1 us
    pallas_call x1, Pallas kernels, per_device(): pl.pallas_call(store, out_shape=[jax.ShapeDtypeStruct(value.shape, BF16)...  1.72 us

profile of v3, /device:TPU:4, one launch (start us, length us, event | category | flops | bytes accessed | tf_op | source)
XLA Modules:
  0.0 47.1 jit_solution(9298597729678793609)
XLA Ops:
  1.3 44.1 %loads.1 = (bf16[1,4,2,384,384]{4,3,2,1,0:T(8,128)(2,1)S(1)}, bf16[1,4,2,128,384]{4,3,2,1,0:T(8,128)(2,1)S(1)}) custom-call(f32[384]{0:T(512)} %freq_hbm.1, f32[384]{0:T(512)} %damp_hbm.1, f32[4]{0:T(128)} %exc_hbm.1, f32[512,384]{1,0:T(8,128)} %bitcast.6, s32[32,96]{1,0:T(8,128)} %attach_hbm.1, s32[1]{0:T(128)S(6)} %copy.10.count_hbm, ...), custom_call_target="tpu_custom_call" | custom-call | tf_op jit(solution)/shard_map/loads/pallas_call | solution.py:266
  45.4 1.7 %store.1 = (bf16[1,4,2,384,384]{4,3,2,1,0:T(8,128)(2,1)}, bf16[1,4,2,128,384]{4,3,2,1,0:T(8,128)(2,1)}) custom-call(bf16[1,4,2,384,384]{4,3,2,1,0:T(8,128)(2,1)S(1)} %get-tuple-element.4.csd_ref, bf16[1,4,2,128,384]{4,3,2,1,0:T(8,128)(2,1)S(1)} %get-tuple-element.5.joint_ref), custom_call_target="tpu_custom_call" | custom-call | tf_op jit(solution)/shard_map/store/pallas_call | solution.py:303

commit v4 on v3

v4 whole, which is shorter than its diff:
```python
import jax
import jax.numpy as jnp
from jax import lax
from jax.experimental import pallas as pl
from jax.experimental.pallas import tpu as pltpu
from jax.sharding import PartitionSpec as P

MESH = pl.DeviceIdType.MESH
F32, BF16 = jnp.float32, jnp.bfloat16
NY, NZ = 4, 8
SIZE = {"y": NY, "z": NZ}
OTHER = {"y": "z", "z": "y"}
COMPS, ATT, LINES, CROSS = 32, 96, 4, 128
PIECES = 4
WAYS = {
    ("z", 4): (((4, 3),), ((3, 2),), ((2, 1),), ((1, 0),)),
    ("z", 3): (((4, 2), (3, 2)), ((2, 1),), ((1, 0),)),
    ("z", 2): (((4, 2), (3, 2), (1, 0)), ((2, 0),)),
    ("z", 1): (((4, 0), (3, 0), (2, 0), (1, 0)),),
    ("y", 2): (((2, 1),), ((1, 0),)),
    ("y", 1): (((2, 0), (1, 0)),),
}
CHUNKS = (
    ("y", 2, 3, 0, 0, 16), ("z", 3, 1, 0, 16, 16), ("y", 2, 2, 0, 32, 8), ("y", 2, 2, 0, 40, 16),
    ("y", 2, 1, 0, 56, 16), ("z", 3, 1, 0, 72, 16), ("z", 3, 1, 0, 88, 8),
)
ORDER = (
    (0, 3, 0), (0, 0, 0), (1, 3, 0), (1, 0, 0), (2, 3, 0), (2, 0, 0), (3, 3, 0), (3, 0, 0), (4, 3, 0),
    (4, 0, 0), (5, 3, 0), (5, 0, 0), (6, 3, 0), (6, 0, 0), (-1, 0, 2), (0, 3, 1), (0, 0, 1), (2, 3, 1),
    (2, 0, 1), (1, 3, 1), (3, 3, 1), (1, 0, 1), (3, 0, 1), (4, 3, 1), (5, 3, 1), (4, 0, 1), (6, 3, 1),
    (0, 3, -1), (1, 3, 2), (2, 3, -1), (3, 3, -1), (5, 0, 1), (5, 3, 2), (4, 3, -1), (6, 3, 2), (6, 3, -1),
    (1, 3, -1), (5, 3, -1), (6, 0, 1), (0, 1, 0), (1, 0, 2), (2, 1, 0), (5, 0, 2), (6, 0, 2), (3, 1, 0),
    (0, 1, 1), (1, 1, 0), (2, 1, 1), (4, 1, 0), (5, 1, 0), (6, 1, 0), (3, 1, 1), (0, 1, 2), (1, 2, 0),
    (2, 2, 0), (5, 2, 0), (6, 2, 0), (4, 2, 0), (0, 2, 0), (3, 2, 0),
)
PAIR = 4
TALL = max(chunk[-1] for chunk in CHUNKS) * PAIR


def axes(index):
    first, way, other_way = CHUNKS[index][:3]
    return ((first, way), (OTHER[first], other_way))


def both_ways(index, stage, k):
    opposite = 2 * k == SIZE[axes(index)[stage][0]]
    return (index % 2,) if stage == 1 and opposite else (0, 1)


def plan():
    place, total = {}, 0
    for index, chunk in enumerate(CHUNKS):
        tall = chunk[-1] * PAIR
        for stage, way in enumerate(axes(index)):
            for k, j in (copy for turn in WAYS[way] for copy in turn):
                size = tall
                if stage == 0:
                    size *= SIZE[OTHER[way[0]]]
                    size //= 2 if 2 * k == SIZE[way[0]] else 1
                for side in both_ways(index, stage, k):
                    place[(index, stage, k, j, side)] = (len(place), total, size)
                    total += size
    return place, total


PLACE, TOTAL = plan()
OWN = [sum(chunk[-1] for chunk in CHUNKS[:index]) * PAIR * COMPS for index in range(len(CHUNKS))]
SLOTS = len(PLACE) + 1 + len(CHUNKS)


def kernel(freq_hbm, damp_hbm, exc_hbm, load_hbm, attach_hbm, count_hbm, otm_hbm, shapes_hbm, csd_ref, joint_ref,
           freq, damp, exc_smem, load, attach, count_smem, otm, shapes, resp, whole, own, held, mine, sent, got,
           otm_got, pick, pick_got, wide, crossing, in_sems, send_sems, recv_sems):
    me = lax.axis_index("mode")
    at = {"y": me // NZ, "z": lax.rem(me, NZ)}

    def device(axis, offset):
        if axis == "z":
            return at["y"] * NZ + lax.rem(at["z"] + offset + NZ, NZ)
        return lax.rem(at["y"] + offset + NY, NY) * NZ + at["z"]

    before = lax.rem(me + NY * NZ - 1, NY * NZ)
    after = lax.rem(me + 1, NY * NZ)
    rows = shapes.shape[0] // PIECES
    parts = [pl.ds(piece * rows, rows) for piece in range(PIECES)]
    halves = [pl.ds(pair * PAIR * 128, PAIR * 128) for pair in range(LINES // PAIR)]
    moves = [(freq_hbm, freq), (damp_hbm, damp), (exc_hbm, exc_smem), (load_hbm.at[halves[0]], load.at[halves[0]])]
    moves += [(shapes_hbm.at[part], shapes.at[part]) for part in parts]
    moves += [(attach_hbm, attach), (otm_hbm, otm), (count_hbm, count_smem)]
    moves += [(load_hbm.at[half], load.at[half]) for half in halves[1:]]
    loads = [pltpu.make_async_copy(src, dst, in_sems.at[k]) for k, (src, dst) in enumerate(moves)]
    for copy in loads:
        copy.start()
    barrier = pltpu.get_barrier_semaphore()
    peers = [device("z", step) for step in range(1, NZ)] + [device("y", step) for step in range(1, NY)]
    for peer in (*peers, before, after):
        pl.semaphore_signal(barrier, inc=1, device_id={"mode": peer}, device_id_type=MESH)
    for copy in loads[:4]:
        copy.wait()
    omega = freq[...].reshape(1, -1)
    ratio = damp[...].reshape(1, -1)
    omega_sq = omega * omega

    def products(pair):
        for line in range(pair * PAIR, pair * PAIR + PAIR):
            exc = exc_smem[line]
            a = omega_sq - exc * exc
            b = 2.0 * ratio * omega * exc
            denom = a * a + b * b
            frf_re = omega_sq * a / denom
            frf_im = -omega_sq * b / denom
            load_re = load[pl.ds(line * 128, 64), :]
            load_im = load[pl.ds(line * 128 + 64, 64), :]
            resp[pl.ds(line * 128, 64), :] = (frf_re * load_re - frf_im * load_im).astype(BF16)
            resp[pl.ds(line * 128 + 64, 64), :] = (frf_re * load_im + frf_im * load_re).astype(BF16)
        for piece in range(PIECES):
            if pair == 0:
                loads[4 + piece].wait()
            block = lax.dot_general(
                shapes[parts[piece], :], resp[halves[pair], :], (((1,), (1,)), ((), ())), preferred_element_type=F32
            )
            for side in range(PAIR):
                place = pl.ds(piece * rows * LINES + pair * PAIR + side, rows, stride=LINES)
                whole[place, :] = block[:, side * 128 : side * 128 + 128]

    products(0)
    loads[4 + PIECES].wait()
    pl.semaphore_wait(barrier, len(peers) + 2)
    copies, tails = {}, [[] for _ in range(LINES // PAIR)]
    table = whole.reshape(whole.shape[0] // LINES, LINES, 128)

    def send(key, place, target, source=sent, dest=got):
        number, offset, size = place
        part = pl.ds(offset, size)
        copy = pltpu.make_async_remote_copy(
            src_ref=source.at[part], dst_ref=dest.at[part], send_sem=send_sems.at[number],
            recv_sem=recv_sems.at[number], device_id={"mode": target}, device_id_type=MESH)
        copy.start()
        copies[key] = copy
        return copy

    def event(index, stage, turn):
        pair, start, rows = CHUNKS[index][3:]
        (first, way), (other, other_way) = axes(index)
        n, m, tall = SIZE[first], SIZE[other], rows * PAIR
        half = m // 2
        home = pl.ds(pair * ATT * PAIR + start * PAIR, tall)

        def block(offset, item):
            return pl.ds(pl.multiple_of(offset + item * tall, 16), tall)

        def gather(dest, item, base):
            unit = item * NZ + dest if first == "z" else dest * NZ + item
            for row in range(rows):
                source = attach[unit, start + row]
                own[pl.ds(base + row * PAIR, PAIR), :] = table[source, pl.ds(pair * PAIR, PAIR), :]

        def arrivals(which, k, side):
            found = [
                (index, which, source, k, side)
                for step in WAYS[axes(index)[which]]
                for source, target in step
                if target == k and side in both_ways(index, which, source)
            ]
            for key in found:
                copies[key].wait_recv()
            return found

        def region(k, side):
            return OWN[index] + (k if side == 0 else (n - k) % n) * m * tall

        if stage == 3:
            kept = [(0, 0, m, 0)]
            for k, side, count, skip in kept if turn < 0 else [
                (k, side, *((half, side * half) if 2 * k == n else (m, 0)))
                for k, _ in WAYS[first, way][turn]
                for side in range(2)
            ]:
                dest = lax.rem(at[first] + (k if side == 0 else n - k), n)

                def body(item, carry):
                    gather(dest, item + skip, pl.multiple_of(region(k, side) + (item + skip) * tall, 16))
                    return carry

                lax.fori_loop(0, count, body, 0)
        elif stage == 0:
            for k, j, side in ((k, j, side) for k, j in WAYS[first, way][turn] for side in range(2)):
                count, skip = (half, side * half) if 2 * k == n else (m, 0)
                place = PLACE[(index, 0, k, j, side)]
                found = arrivals(0, k, side)
                short = [PLACE[key][1] for key in found if 2 * key[2] == n]
                full = [PLACE[key][1] for key in found if 2 * key[2] != n]

                def put(item, partly):
                    value = own[block(region(k, side), item + skip), :]
                    for offset in full:
                        value = value + got[block(offset, item), :].astype(F32)
                    for offset in short if partly is not None else ():
                        value = value + got[block(offset, partly), :].astype(F32)
                    sent[block(place[1], item), :] = value.astype(BF16)

                if short:
                    def fill(item, carry):
                        put(side * half + item, item)
                        put((1 - side) * half + item, None)
                        return carry

                    lax.fori_loop(0, half, fill, 0)
                else:
                    def fill(item, carry):
                        put(item, None)
                        return carry

                    lax.fori_loop(0, count, fill, 0)
                send((index, 0, k, j, side), place, device(first, k - j if side == 0 else j - k))
        elif stage == 1 and turn == 0:
            arrived = [PLACE[key][1] for side in range(2) for key in arrivals(0, 0, side)]

            def value(item):
                here = own[block(region(0, 0), item), :]
                for offset in arrived:
                    here = here + got[block(offset, item), :].astype(F32)
                return here

            targets = dict(WAYS[other, other_way][0])
            for k in (*sorted(targets, reverse=True), *(k for k in range(1, half + 1) if k not in targets)):
                for side in both_ways(index, 1, k):
                    here = value(lax.rem(at[other] + (k if side == 0 else m - k), m))
                    if k in targets:
                        j = targets[k]
                        place = PLACE[(index, 1, k, j, side)]
                        sent[pl.ds(place[1], tall), :] = here.astype(BF16)
                        send((index, 1, k, j, side), place, device(other, k - j if side == 0 else j - k))
                    else:
                        held[pl.ds(((index * half + k - 1) * 2 + side) * TALL, tall), :] = here
            mine[home, :] = value(at[other])
        elif stage == 1:
            for k, j in WAYS[other, other_way][turn]:
                for side in both_ways(index, 1, k):
                    here = held[pl.ds(((index * half + k - 1) * 2 + side) * TALL, tall), :]
                    for key in arrivals(1, k, side):
                        here = here + got[pl.ds(PLACE[key][1], tall), :].astype(F32)
                    place = PLACE[(index, 1, k, j, side)]
                    sent[pl.ds(place[1], tall), :] = here.astype(BF16)
                    send((index, 1, k, j, side), place, device(other, k - j if side == 0 else j - k))
        else:
            here = mine[home, :]
            for side in range(2):
                for key in arrivals(1, 0, side):
                    here = here + got[pl.ds(PLACE[key][1], tall), :].astype(F32)
            pick[home, :] = here.astype(BF16)
            place = (len(PLACE) + 1 + index, pair * ATT * PAIR + start * PAIR, tall)
            tails[pair].append(send((index, "pick"), place, before, pick, pick_got))

    def factor(otm_ref, side):
        picked = wide[pl.ds(side, ATT, stride=PAIR), :].astype(BF16)
        return lax.dot_general(
            otm_ref[...], picked, (((0,), (0,)), ((), ())), preferred_element_type=F32
        ).astype(BF16)

    def spectra(left, right):
        return lax.dot_general(left, right, (((1,), (1,)), ((), ())), preferred_element_type=F32) * (1.0 / 64.0)

    def direct(pair):
        wide[...] = pick[pl.ds(pair * ATT * PAIR, ATT * PAIR), :].astype(F32)
        for side in range(PAIR):
            line = pair * PAIR + side
            here = factor(otm, side)
            lane = lax.broadcasted_iota(jnp.int32, here.shape, 1)
            turned = pltpu.roll(here.astype(F32), 64, 1)
            turned = jnp.where(lane < 64, turned, -turned).astype(BF16)
            csd_ref[0, line, 0] = spectra(here, here).astype(BF16)
            csd_ref[0, line, 1] = spectra(turned, here).astype(BF16)
            crossing[line, 0] = here[:CROSS]
            crossing[line, 1] = turned[:CROSS]

    def joint(pair):
        for copy in tails[pair]:
            copy.wait_recv()
        arrived = pick_got[pl.ds(pair * ATT * PAIR, ATT * PAIR), :].astype(F32)
        wide[...] = jnp.where(me == NY * NZ - 1, 0.0, arrived)
        for side in range(PAIR):
            line = pair * PAIR + side
            following = factor(otm_got, side)
            for part in range(2):
                joint_ref[0, line, part] = spectra(crossing[line, part], following).astype(BF16)

    for index, stage, turn in ORDER:
        if index >= 0:
            event(index, stage, turn)
        elif turn == 0:
            loads[7 + PIECES].wait()
            products(1)
        elif turn == 1:
            direct(0)
        else:
            loads[5 + PIECES].wait()
            loads[6 + PIECES].wait()
            keep = lax.broadcasted_iota(jnp.int32, otm.shape, 1) < count_smem[0]
            otm[...] = jnp.where(keep, otm[...].astype(F32), 0.0).astype(BF16)
            otm_copy = pltpu.make_async_remote_copy(
                src_ref=otm, dst_ref=otm_got, send_sem=send_sems.at[len(PLACE)],
                recv_sem=recv_sems.at[len(PLACE)], device_id={"mode": before}, device_id_type=MESH)
            otm_copy.start()
    direct(LINES // PAIR - 1)
    otm_copy.wait_recv()
    for pair in range(LINES // PAIR):
        joint(pair)
    for copy in (*copies.values(), otm_copy):
        copy.wait_send()


def store(csd_ref, joint_ref, csd_hbm, joint_hbm, sems):
    copies = []
    for line in range(LINES):
        copies.append(pltpu.make_async_copy(csd_ref.at[0, line], csd_hbm.at[0, line], sems.at[2 * line]))
        copies.append(pltpu.make_async_copy(joint_ref.at[0, line], joint_hbm.at[0, line], sems.at[2 * line + 1]))
    for copy in copies:
        copy.start()
    for copy in copies:
        copy.wait()


def per_device(mode_shapes, modal_freq, damping, excitation, modal_load, attach, row_count, otm):
    iface, modes = mode_shapes.shape
    rows_max, width = otm.shape[1], modal_load.shape[3]
    columns = LINES * 2 * width
    vmem = pl.BlockSpec(memory_space=pltpu.VMEM)
    hbm = pl.BlockSpec(memory_space=pltpu.HBM)
    operands = (
        modal_freq,
        damping,
        excitation,
        modal_load.transpose(1, 2, 3, 0).reshape(columns, modes),
        attach,
        row_count,
        otm[0].T,
        mode_shapes,
    )
    spectra = pl.pallas_call(
            kernel,
            out_shape=[
                jax.ShapeDtypeStruct((1, LINES, 2, rows_max, rows_max), BF16),
                jax.ShapeDtypeStruct((1, LINES, 2, CROSS, rows_max), BF16),
            ],
            in_specs=[hbm] * 8,
            out_specs=[vmem] * 2,
            scratch_shapes=[
                pltpu.VMEM((modes,), F32),
                pltpu.VMEM((modes,), F32),
                pltpu.SMEM((LINES,), F32),
                pltpu.VMEM((columns, modes), F32),
                pltpu.SMEM((COMPS, ATT), jnp.int32),
                pltpu.SMEM((1,), jnp.int32),
                pltpu.VMEM((ATT, rows_max), BF16),
                pltpu.VMEM((iface, modes), BF16),
                pltpu.VMEM((columns, modes), BF16),
                pltpu.VMEM((iface * LINES, 128), F32),
                pltpu.VMEM((COMPS * ATT * LINES, 128), F32),
                pltpu.VMEM((len(CHUNKS) * NZ * TALL, 128), F32),
                pltpu.VMEM((ATT * LINES, 128), F32),
                pltpu.VMEM((TOTAL, 128), BF16),
                pltpu.VMEM((TOTAL, 128), BF16),
                pltpu.VMEM((ATT, rows_max), BF16),
                pltpu.VMEM((ATT * LINES, 128), BF16),
                pltpu.VMEM((ATT * LINES, 128), BF16),
                pltpu.VMEM((ATT * PAIR, 128), F32),
                pltpu.VMEM((LINES, 2, CROSS, 128), BF16),
                pltpu.SemaphoreType.DMA((8 + PIECES,)),
                pltpu.SemaphoreType.DMA((SLOTS,)),
                pltpu.SemaphoreType.DMA((SLOTS,)),
            ],
            compiler_params=pltpu.CompilerParams(
                vmem_limit_bytes=42 << 20, collective_id=0, has_side_effects=True
            ),
            name="loads",
        )(*(value if value is row_count else pltpu.with_memory_space_constraint(value, pltpu.HBM) for value in operands))
    return tuple(
        pl.pallas_call(
            store,
            out_shape=[jax.ShapeDtypeStruct(value.shape, BF16) for value in spectra],
            in_specs=[vmem] * 2,
            out_specs=[hbm] * 2,
            scratch_shapes=[pltpu.SemaphoreType.DMA((2 * LINES,))],
            compiler_params=pltpu.CompilerParams(vmem_limit_bytes=1 << 20),
            name="store",
        )(*spectra)
    )


def solution(mesh):
    return jax.shard_map(
        per_device,
        mesh=mesh,
        in_specs=(
            P(None, "mode"),
            P("mode"),
            P("mode"),
            P("freq"),
            P("mode", "freq", None, None),
            P(),
            P("mode"),
            P("mode", None, None),
        ),
        out_specs=(P("mode", "freq", None, None, None), P("mode", "freq", None, None, None)),
        check_vma=False,
    )
```

time: 47.2 us -> 44.2 us (0.936)
  Pallas kernels: 45.8 us -> 42.7 us
    pallas_call x1, Pallas kernels: 44.1 us -> 41 us  [per_device(): pl.pallas_call(kernel, out_shape=[jax.ShapeDtypeStruct((1, LINES, 2, rows...]
where the time goes in v4:
time: 44.2 us; the launch traced here: 44 us
  Pallas kernels  42.7 us (97%)
  between operations  1.29 us (3%)
    pallas_call x1, Pallas kernels, per_device(): pl.pallas_call(kernel, out_shape=[jax.ShapeDtypeStruct((1, LINES, 2, rows...  41 us
    pallas_call x1, Pallas kernels, per_device(): pl.pallas_call(store, out_shape=[jax.ShapeDtypeStruct(value.shape, BF16)...  1.72 us

profile of v4, /device:TPU:4, one launch (start us, length us, event | category | flops | bytes accessed | tf_op | source)
XLA Modules:
  0.0 44.0 jit_solution(1681222609270082673)
XLA Ops:
  1.3 41.0 %loads.1 = (bf16[1,4,2,384,384]{4,3,2,1,0:T(8,128)(2,1)S(1)}, bf16[1,4,2,128,384]{4,3,2,1,0:T(8,128)(2,1)S(1)}) custom-call(f32[384]{0:T(512)} %freq_hbm.1, f32[384]{0:T(512)} %damp_hbm.1, f32[4]{0:T(128)} %exc_hbm.1, f32[512,384]{1,0:T(8,128)} %bitcast.6, s32[32,96]{1,0:T(8,128)} %attach_hbm.1, s32[1]{0:T(128)S(6)} %copy.10.count_hbm, ...), custom_call_target="tpu_custom_call" | custom-call | tf_op jit(solution)/shard_map/loads/pallas_call | solution.py:340
  42.2 1.7 %store.1 = (bf16[1,4,2,384,384]{4,3,2,1,0:T(8,128)(2,1)}, bf16[1,4,2,128,384]{4,3,2,1,0:T(8,128)(2,1)}) custom-call(bf16[1,4,2,384,384]{4,3,2,1,0:T(8,128)(2,1)S(1)} %get-tuple-element.4.csd_ref, bf16[1,4,2,128,384]{4,3,2,1,0:T(8,128)(2,1)S(1)} %get-tuple-element.5.joint_ref), custom_call_target="tpu_custom_call" | custom-call | tf_op jit(solution)/shard_map/store/pallas_call | solution.py:379

commit v5 on v4

--- a/solution.py
+++ b/solution.py
@@ -11,7 +11,8 @@
 SIZE = {"y": NY, "z": NZ}
 OTHER = {"y": "z", "z": "y"}
 COMPS, ATT, LINES, CROSS = 32, 96, 4, 128
-PIECES = 4
+CUTS = (0, 768, 2304, 4224, 6144)
+PIECES = len(CUTS) - 1
 WAYS = {
     ("z", 4): (((4, 3),), ((3, 2),), ((2, 1),), ((1, 0),)),
     ("z", 3): (((4, 2), (3, 2)), ((2, 1),), ((1, 0),)),
@@ -81,8 +82,7 @@
 
     before = lax.rem(me + NY * NZ - 1, NY * NZ)
     after = lax.rem(me + 1, NY * NZ)
-    rows = shapes.shape[0] // PIECES
-    parts = [pl.ds(piece * rows, rows) for piece in range(PIECES)]
+    parts = [pl.ds(low, high - low) for low, high in zip(CUTS, CUTS[1:])]
     halves = [pl.ds(pair * PAIR * 128, PAIR * 128) for pair in range(LINES // PAIR)]
     moves = [(freq_hbm, freq), (damp_hbm, damp), (exc_hbm, exc_smem), (load_hbm.at[halves[0]], load.at[halves[0]])]
     moves += [(shapes_hbm.at[part], shapes.at[part]) for part in parts]
@@ -111,16 +111,16 @@
             frf_im = -omega_sq * b / denom
             load_re = load[pl.ds(line * 128, 64), :]
             load_im = load[pl.ds(line * 128 + 64, 64), :]
-            resp[pl.ds(line * 128, 64), :] = (frf_re * load_re - frf_im * load_im).astype(BF16)
-            resp[pl.ds(line * 128 + 64, 64), :] = (frf_re * load_im + frf_im * load_re).astype(BF16)
+            parted = [frf_re * load_re - frf_im * load_im, frf_re * load_im + frf_im * load_re]
+            resp[:, pl.ds(line * 128, 128)] = jnp.concatenate(parted, axis=0).astype(BF16).T
         for piece in range(PIECES):
             if pair == 0:
                 loads[4 + piece].wait()
             block = lax.dot_general(
-                shapes[parts[piece], :], resp[halves[pair], :], (((1,), (1,)), ((), ())), preferred_element_type=F32
+                shapes[parts[piece], :], resp[:, halves[pair]], (((1,), (0,)), ((), ())), preferred_element_type=F32
             )
             for side in range(PAIR):
-                place = pl.ds(piece * rows * LINES + pair * PAIR + side, rows, stride=LINES)
+                place = pl.ds(CUTS[piece] * LINES + pair * PAIR + side, CUTS[piece + 1] - CUTS[piece], stride=LINES)
                 whole[place, :] = block[:, side * 128 : side * 128 + 128]
 
     products(0)
@@ -354,7 +354,7 @@
                 pltpu.SMEM((1,), jnp.int32),
                 pltpu.VMEM((ATT, rows_max), BF16),
                 pltpu.VMEM((iface, modes), BF16),
-                pltpu.VMEM((columns, modes), BF16),
+                pltpu.VMEM((modes, columns), BF16),
                 pltpu.VMEM((iface * LINES, 128), F32),
                 pltpu.VMEM((COMPS * ATT * LINES, 128), F32),
                 pltpu.VMEM((len(CHUNKS) * NZ * TALL, 128), F32),

time: 44.2 us -> 43.9 us (level)
  no operation moved by 1% of the time
where the time goes in v5:
time: 43.9 us; the launch traced here: 43.6 us
  Pallas kernels  42.4 us (97%)
  between operations  1.29 us (3%)
    pallas_call x1, Pallas kernels, per_device(): pl.pallas_call(kernel, out_shape=[jax.ShapeDtypeStruct((1, LINES, 2, rows...  40.6 us
    pallas_call x1, Pallas kernels, per_device(): pl.pallas_call(store, out_shape=[jax.ShapeDtypeStruct(value.shape, BF16)...  1.72 us

profile of v5, /device:TPU:4, one launch (start us, length us, event | category | flops | bytes accessed | tf_op | source)
XLA Modules:
  0.0 43.6 jit_solution(18157808544411753391)
XLA Ops:
  1.3 40.6 %loads.1 = (bf16[1,4,2,384,384]{4,3,2,1,0:T(8,128)(2,1)S(1)}, bf16[1,4,2,128,384]{4,3,2,1,0:T(8,128)(2,1)S(1)}) custom-call(f32[384]{0:T(512)} %freq_hbm.1, f32[384]{0:T(512)} %damp_hbm.1, f32[4]{0:T(128)} %exc_hbm.1, f32[512,384]{1,0:T(8,128)} %bitcast.6, s32[32,96]{1,0:T(8,128)} %attach_hbm.1, s32[1]{0:T(128)S(6)} %copy.10.count_hbm, ...), custom_call_target="tpu_custom_call" | custom-call | tf_op jit(solution)/shard_map/loads/pallas_call | solution.py:340
  41.9 1.7 %store.1 = (bf16[1,4,2,384,384]{4,3,2,1,0:T(8,128)(2,1)}, bf16[1,4,2,128,384]{4,3,2,1,0:T(8,128)(2,1)}) custom-call(bf16[1,4,2,384,384]{4,3,2,1,0:T(8,128)(2,1)S(1)} %get-tuple-element.4.csd_ref, bf16[1,4,2,128,384]{4,3,2,1,0:T(8,128)(2,1)S(1)} %get-tuple-element.5.joint_ref), custom_call_target="tpu_custom_call" | custom-call | tf_op jit(solution)/shard_map/store/pallas_call | solution.py:379

commit v6 on v5

--- a/solution.py
+++ b/solution.py
@@ -22,17 +22,17 @@
     ("y", 1): (((2, 0), (1, 0)),),
 }
 CHUNKS = (
-    ("y", 2, 3, 0, 0, 16), ("z", 3, 1, 0, 16, 16), ("y", 2, 2, 0, 32, 8), ("y", 2, 2, 0, 40, 16),
-    ("y", 2, 1, 0, 56, 16), ("z", 3, 1, 0, 72, 16), ("z", 3, 1, 0, 88, 8),
+    ("z", 4, 1, 0, 0, 16), ("y", 2, 3, 0, 16, 16), ("z", 3, 1, 0, 32, 16), ("z", 4, 1, 0, 48, 16),
+    ("y", 2, 2, 0, 64, 16), ("y", 2, 1, 0, 80, 16),
 )
 ORDER = (
-    (0, 3, 0), (0, 0, 0), (1, 3, 0), (1, 0, 0), (2, 3, 0), (2, 0, 0), (3, 3, 0), (3, 0, 0), (4, 3, 0),
-    (4, 0, 0), (5, 3, 0), (5, 0, 0), (6, 3, 0), (6, 0, 0), (-1, 0, 2), (0, 3, 1), (0, 0, 1), (2, 3, 1),
-    (2, 0, 1), (1, 3, 1), (3, 3, 1), (1, 0, 1), (3, 0, 1), (4, 3, 1), (5, 3, 1), (4, 0, 1), (6, 3, 1),
-    (0, 3, -1), (1, 3, 2), (2, 3, -1), (3, 3, -1), (5, 0, 1), (5, 3, 2), (4, 3, -1), (6, 3, 2), (6, 3, -1),
-    (1, 3, -1), (5, 3, -1), (6, 0, 1), (0, 1, 0), (1, 0, 2), (2, 1, 0), (5, 0, 2), (6, 0, 2), (3, 1, 0),
-    (0, 1, 1), (1, 1, 0), (2, 1, 1), (4, 1, 0), (5, 1, 0), (6, 1, 0), (3, 1, 1), (0, 1, 2), (1, 2, 0),
-    (2, 2, 0), (5, 2, 0), (6, 2, 0), (4, 2, 0), (0, 2, 0), (3, 2, 0),
+    (0, 3, 0), (0, 0, 0), (1, 3, 0), (1, 0, 0), (3, 3, 0), (3, 0, 0), (2, 3, 0), (2, 0, 0), (4, 3, 0),
+    (4, 0, 0), (5, 3, 0), (5, 0, 0), (-1, 0, 2), (0, 3, 1), (3, 3, 1), (1, 3, 1), (0, 0, 1), (4, 3, 1),
+    (2, 3, 1), (3, 0, 1), (1, 0, 1), (5, 3, 1), (0, 3, 2), (3, 3, 2), (1, 3, -1), (4, 3, -1), (4, 0, 1),
+    (2, 0, 1), (2, 3, 2), (5, 3, -1), (5, 0, 1), (0, 0, 2), (0, 3, 3), (3, 3, 3), (3, 3, -1), (2, 3, -1),
+    (0, 3, -1), (3, 0, 2), (1, 1, 0), (2, 0, 2), (0, 0, 3), (4, 1, 0), (3, 0, 3), (1, 1, 1), (5, 1, 0),
+    (2, 1, 0), (0, 1, 0), (4, 1, 1), (3, 1, 0), (1, 1, 2), (2, 2, 0), (0, 2, 0), (5, 2, 0), (1, 2, 0),
+    (4, 2, 0), (3, 2, 0),
 )
 PAIR = 4
 TALL = max(chunk[-1] for chunk in CHUNKS) * PAIR

time: 43.9 us -> 44 us (level)
  no operation moved by 1% of the time
where the time goes in v6:
time: 44 us; the launch traced here: 43.5 us
  Pallas kernels  42.2 us (96%)
  between operations  1.29 us (3%)
    pallas_call x1, Pallas kernels, per_device(): pl.pallas_call(kernel, out_shape=[jax.ShapeDtypeStruct((1, LINES, 2, rows...  40.5 us
    pallas_call x1, Pallas kernels, per_device(): pl.pallas_call(store, out_shape=[jax.ShapeDtypeStruct(value.shape, BF16)...  1.72 us

profile of v6, /device:TPU:4, one launch (start us, length us, event | category | flops | bytes accessed | tf_op | source)
XLA Modules:
  0.0 43.5 jit_solution(5929794411262286608)
XLA Ops:
  1.3 40.5 %loads.1 = (bf16[1,4,2,384,384]{4,3,2,1,0:T(8,128)(2,1)S(1)}, bf16[1,4,2,128,384]{4,3,2,1,0:T(8,128)(2,1)S(1)}) custom-call(f32[384]{0:T(512)} %freq_hbm.1, f32[384]{0:T(512)} %damp_hbm.1, f32[4]{0:T(128)} %exc_hbm.1, f32[512,384]{1,0:T(8,128)} %bitcast.6, s32[32,96]{1,0:T(8,128)} %attach_hbm.1, s32[1]{0:T(128)S(6)} %copy.10.count_hbm, ...), custom_call_target="tpu_custom_call" | custom-call | tf_op jit(solution)/shard_map/loads/pallas_call | solution.py:340
  41.8 1.7 %store.1 = (bf16[1,4,2,384,384]{4,3,2,1,0:T(8,128)(2,1)}, bf16[1,4,2,128,384]{4,3,2,1,0:T(8,128)(2,1)}) custom-call(bf16[1,4,2,384,384]{4,3,2,1,0:T(8,128)(2,1)S(1)} %get-tuple-element.4.csd_ref, bf16[1,4,2,128,384]{4,3,2,1,0:T(8,128)(2,1)S(1)} %get-tuple-element.5.joint_ref), custom_call_target="tpu_custom_call" | custom-call | tf_op jit(solution)/shard_map/store/pallas_call | solution.py:379
